TPU v7x, 32 devices: a whole 2x2x4 slice. The times are simulated.
32 devices in a mesh: fsdp: 32 (over z, y, x, core).
Axes of the slice: x: 2, y: 2, z: 4, core: 2. Of those that a mesh axis runs over, the one named last changes fastest.
Arguments:
- tokens: bfloat16 [512, 64, 768], P('fsdp'), may hold values from -6 to 6
- lengths: int32 [512], P('fsdp'), may hold values from 3 to 64, as said below
- partners: int32 [256], P('fsdp'), may hold values from 0 to 255, each once
- out_cotangent: bfloat16 [512, 64, 768], P('fsdp'), may hold values from -6 to 6
- w_query: bfloat16 [768, 768], P('fsdp'), may hold values from -0.21875 to 0.21875
- w_key: bfloat16 [768, 768], P('fsdp'), may hold values from -0.21875 to 0.21875
- w_value: bfloat16 [768, 768], P('fsdp'), may hold values from -0.21875 to 0.21875
- w_output: bfloat16 [768, 768], P('fsdp'), may hold values from -0.625 to 0.625
- b_query: bfloat16 [768], P('fsdp'), may hold values from -1.5 to 1.5
- b_value: bfloat16 [768], P('fsdp'), may hold values from -1.5 to 1.5
- b_output: bfloat16 [768], P('fsdp'), may hold values from -1.5 to 1.5
- gain_attn: bfloat16 [768], P('fsdp'), may hold values from 0.5 to 1.5
- shift_attn: bfloat16 [768], P('fsdp'), may hold values from -1.5 to 1.5
- w_inner: bfloat16 [768, 3072], P('fsdp'), may hold values from -0.21875 to 0.21875
- b_inner: bfloat16 [3072], P('fsdp'), may hold values from -1.5 to 1.5
- w_outer: bfloat16 [3072, 768], P('fsdp'), may hold values from -0.15625 to 0.15625
- b_outer: bfloat16 [768], P('fsdp'), may hold values from -1.5 to 1.5
- gain_ffn: bfloat16 [768], P('fsdp'), may hold values from 0.5 to 1.5
- shift_ffn: bfloat16 [768], P('fsdp'), may hold values from -1.5 to 1.5
Outputs:
- loss: float32 [], replicated
- block_out: bfloat16 [512, 64, 768], P('fsdp')
- grad_tokens: float32 [512, 64, 768], P('fsdp')
- grad_w_query: float32 [768, 768], P('fsdp')
- grad_w_key: float32 [768, 768], P('fsdp')
- grad_w_value: float32 [768, 768], P('fsdp')
- grad_w_output: float32 [768, 768], P('fsdp')
- grad_b_query: float32 [768], P('fsdp')
- grad_b_value: float32 [768], P('fsdp')
- grad_b_output: float32 [768], P('fsdp')
- grad_gain_attn: float32 [768], P('fsdp')
- grad_shift_attn: float32 [768], P('fsdp')
- grad_w_inner: float32 [768, 3072], P('fsdp')
- grad_b_inner: float32 [3072], P('fsdp')
- grad_w_outer: float32 [3072, 768], P('fsdp')
- grad_b_outer: float32 [768], P('fsdp')
- grad_gain_ffn: float32 [768], P('fsdp')
- grad_shift_ffn: float32 [768], P('fsdp')
Inputs may be any that keep to these rules, and one draw needn't show every extreme that they name: `lengths`: each sentence slot has 3 to 64 live tokens, heavy toward short ones; at least one slot has 64.
All inputs are finite; a program needn't handle non-finite values.
Results may differ from a plain program's by a relative error of at most 0.013.
Values may be sent and summed in bfloat16 or wider, within the bound.
No kernel may reach another device: no remote copies, remote signals or barrier semaphores. Data moves between devices by JAX's collectives and lax.ppermute only.
A program may use at most 192 MiB of HBM per device.

v0:
```python
import jax
import jax.numpy as jnp
from jax import lax
from jax.sharding import PartitionSpec as P

D = 768
HEADS = 12
HEAD_DIM = 64
LEN = 64
norm_eps = 1e-12
pool_eps = 1e-06
sim_scale = 50.0
sim_margin = 0.3


def project(rows, weight):
    return jnp.dot(rows, weight, preferred_element_type=jnp.float32)


def project_back(grad, weight):
    return lax.dot_general(
        grad, weight, (((1,), (1,)), ((), ())), preferred_element_type=jnp.float32
    )


def weight_grad(rows, grad):
    return lax.dot_general(rows, grad, (((0,), (0,)), ((), ())), preferred_element_type=jnp.float32)


def scaled_norm(field, gain_vec):
    centred = field - jnp.mean(field, axis=-1, keepdims=True)
    variance = jnp.mean(centred * centred, axis=-1, keepdims=True)
    return centred * lax.rsqrt(variance + norm_eps) * gain_vec


def exact_gelu(field):
    return jax.nn.gelu(field, approximate=False)


def normalize(field):
    return field * lax.rsqrt(jnp.sum(field * field, axis=-1, keepdims=True) + pool_eps)


def scores_of(queries, key_rows, visible):
    raw = jnp.einsum(
        "bqhd,bkhd->bhqk", queries, key_rows, preferred_element_type=jnp.float32
    ) * HEAD_DIM ** (-0.5)
    return jnp.where(visible, raw, -1e30)


def column_sum(field):
    return jnp.sum(field.astype(jnp.float32), axis=0)


def local(
    tokens,
    lengths,
    partners,
    out_cotangent,
    w_query,
    w_key,
    w_value,
    w_output,
    b_query,
    b_value,
    b_output,
    gain_attn,
    shift_attn,
    w_inner,
    b_inner,
    w_outer,
    b_outer,
    gain_ffn,
    shift_ffn,
):
    count = tokens.shape[0]
    half = count // 2
    shape_four = (count, LEN, HEADS, HEAD_DIM)
    token_rows = tokens.reshape(count * LEN, D)
    positions = jnp.arange(LEN, dtype=jnp.int32)
    visible = (positions[None, :] < lengths[:, None])[:, None, None, :]
    attn_full = (
        lax.all_gather(w_query, "fsdp", axis=0, tiled=True),
        lax.all_gather(w_key, "fsdp", axis=0, tiled=True),
        lax.all_gather(w_value, "fsdp", axis=0, tiled=True),
        lax.all_gather(w_output, "fsdp", axis=0, tiled=True),
        lax.all_gather(b_query, "fsdp", axis=0, tiled=True),
        lax.all_gather(b_value, "fsdp", axis=0, tiled=True),
        lax.all_gather(b_output, "fsdp", axis=0, tiled=True),
        lax.all_gather(gain_attn, "fsdp", axis=0, tiled=True),
        lax.all_gather(shift_attn, "fsdp", axis=0, tiled=True),
    )
    (
        query_mat,
        key_mat,
        value_mat,
        output_mat,
        query_bias,
        value_bias,
        output_bias,
        attn_gain,
        attn_shift,
    ) = attn_full
    queries = (project(token_rows, query_mat) + query_bias).astype(jnp.bfloat16).reshape(shape_four)
    key_rows = project(token_rows, key_mat).astype(jnp.bfloat16).reshape(shape_four)
    value_rows = (
        (project(token_rows, value_mat) + value_bias).astype(jnp.bfloat16).reshape(shape_four)
    )
    scores = scores_of(queries, key_rows, visible)
    row_top = jnp.max(scores, axis=-1, keepdims=True)
    expd = jnp.exp(scores - row_top)
    row_total = jnp.sum(expd, axis=-1, keepdims=True)
    probs = expd / row_total
    score_lse = row_top + jnp.log(row_total)
    context = jnp.einsum(
        "bhqk,bkhd->bqhd",
        probs.astype(jnp.bfloat16),
        value_rows,
        preferred_element_type=jnp.float32,
    )
    context = context.astype(jnp.bfloat16).reshape(count * LEN, D)
    resid_attn = token_rows.astype(jnp.float32) + (project(context, output_mat) + output_bias)
    normed_attn = scaled_norm(resid_attn, attn_gain.astype(jnp.float32)) + attn_shift
    ffn_full = (
        lax.all_gather(w_inner, "fsdp", axis=0, tiled=True),
        lax.all_gather(b_inner, "fsdp", axis=0, tiled=True),
        lax.all_gather(w_outer, "fsdp", axis=0, tiled=True),
        lax.all_gather(b_outer, "fsdp", axis=0, tiled=True),
        lax.all_gather(gain_ffn, "fsdp", axis=0, tiled=True),
        lax.all_gather(shift_ffn, "fsdp", axis=0, tiled=True),
    )
    inner_mat, inner_bias, outer_mat, outer_bias, ffn_gain, ffn_shift = ffn_full
    normed_low = normed_attn.astype(jnp.bfloat16)
    hidden_pre = project(normed_low, inner_mat) + inner_bias
    hidden_act = exact_gelu(hidden_pre).astype(jnp.bfloat16)
    resid_ffn = normed_attn + (project(hidden_act, outer_mat) + outer_bias)
    block_rows = scaled_norm(resid_ffn, ffn_gain.astype(jnp.float32)) + ffn_shift
    block_out = block_rows.astype(jnp.bfloat16).reshape(count, LEN, D)
    cls_rows = block_rows.reshape(count, LEN, D)[:, 0, :]
    unit, pool_back = jax.vjp(normalize, cls_rows)
    unit_low = unit.astype(jnp.bfloat16)
    every_unit = lax.all_gather(unit_low, "fsdp", axis=0, tiled=True)
    every_pair = every_unit.reshape(every_unit.shape[0] // 2, 2, D)
    all_targets = every_pair[:, 1, :]
    own_pair = unit_low.reshape(half, 2, D)
    own_sources = own_pair[:, 0, :]
    npairs = all_targets.shape[0]
    sims = project_back(own_sources, all_targets) * sim_scale
    matched = partners[:, None] == jnp.arange(npairs, dtype=jnp.int32)[None, :]
    sims = sims - jnp.where(matched, sim_scale * sim_margin, 0.0)
    sim_top = jnp.max(sims, axis=1, keepdims=True)
    row_lse = sim_top + jnp.log(jnp.sum(jnp.exp(sims - sim_top), axis=1, keepdims=True))
    col_part = jnp.sum(jnp.exp(sims - sim_scale), axis=0)
    positive = jnp.sum(jnp.where(matched, sims, 0.0))
    local_loss = jnp.sum(row_lse) - 2.0 * positive
    col_total, loss_total = lax.psum((col_part, local_loss), "fsdp")
    col_lse = sim_scale + jnp.log(col_total)
    loss = (loss_total + jnp.sum(col_lse)) / (2.0 * npairs)
    d_sims = 0.5 * (jnp.exp(sims - row_lse) + jnp.exp(sims - col_lse[None, :])) - jnp.where(
        matched, 1.0, 0.0
    )
    d_sims_low = (d_sims * sim_scale).astype(jnp.bfloat16)
    d_source = project(d_sims_low, all_targets)
    target_part = weight_grad(d_sims_low, own_sources)
    d_target = lax.psum_scatter(target_part, "fsdp", scatter_dimension=0, tiled=True)
    d_unit = jnp.stack([d_source, d_target], axis=1).reshape(count, D)
    (d_cls,) = pool_back(d_unit)
    d_block = out_cotangent.astype(jnp.float32).at[:, 0, :].add(d_cls).reshape(count * LEN, D)
    inner_back, outer_back, ffn_gain_back = (
        lax.all_gather(w_inner, "fsdp", axis=0, tiled=True),
        lax.all_gather(w_outer, "fsdp", axis=0, tiled=True),
        lax.all_gather(gain_ffn, "fsdp", axis=0, tiled=True),
    )
    _, ffn_norm_back = jax.vjp(scaled_norm, resid_ffn, ffn_gain_back.astype(jnp.float32))
    d_resid_ffn, d_ffn_gain = ffn_norm_back(d_block)
    d_ffn_shift = jnp.sum(d_block, axis=0)
    d_branch = d_resid_ffn.astype(jnp.bfloat16)
    d_outer_bias = column_sum(d_branch)
    d_outer_mat = weight_grad(hidden_act, d_branch)
    d_act = project_back(d_branch, outer_back)
    _, gelu_back = jax.vjp(exact_gelu, hidden_pre)
    (d_pre,) = gelu_back(d_act)
    d_hidden = d_pre.astype(jnp.bfloat16)
    d_inner_mat = weight_grad(normed_low, d_hidden)
    d_inner_bias = column_sum(d_hidden)
    d_normed = d_resid_ffn + project_back(d_hidden, inner_back)
    grad_w_inner, grad_b_inner, grad_w_outer, grad_b_outer, grad_gain_ffn, grad_shift_ffn = (
        lax.psum_scatter(d_inner_mat, "fsdp", scatter_dimension=0, tiled=True),
        lax.psum_scatter(d_inner_bias, "fsdp", scatter_dimension=0, tiled=True),
        lax.psum_scatter(d_outer_mat, "fsdp", scatter_dimension=0, tiled=True),
        lax.psum_scatter(d_outer_bias, "fsdp", scatter_dimension=0, tiled=True),
        lax.psum_scatter(d_ffn_gain, "fsdp", scatter_dimension=0, tiled=True),
        lax.psum_scatter(d_ffn_shift, "fsdp", scatter_dimension=0, tiled=True),
    )
    query_back, key_back, value_back, output_back, attn_gain_back = (
        lax.all_gather(w_query, "fsdp", axis=0, tiled=True),
        lax.all_gather(w_key, "fsdp", axis=0, tiled=True),
        lax.all_gather(w_value, "fsdp", axis=0, tiled=True),
        lax.all_gather(w_output, "fsdp", axis=0, tiled=True),
        lax.all_gather(gain_attn, "fsdp", axis=0, tiled=True),
    )
    _, attn_norm_back = jax.vjp(scaled_norm, resid_attn, attn_gain_back.astype(jnp.float32))
    d_resid_attn, d_attn_gain = attn_norm_back(d_normed)
    d_attn_shift = jnp.sum(d_normed, axis=0)
    d_attn_out = d_resid_attn.astype(jnp.bfloat16)
    d_output_bias = column_sum(d_attn_out)
    d_output_mat = weight_grad(context, d_attn_out)
    d_context = project_back(d_attn_out, output_back).astype(jnp.bfloat16).reshape(shape_four)
    probs_again = jnp.exp(scores_of(queries, key_rows, visible) - score_lse)
    d_probs = jnp.einsum(
        "bqhd,bkhd->bhqk", d_context, value_rows, preferred_element_type=jnp.float32
    )
    d_values = jnp.einsum(
        "bhqk,bqhd->bkhd",
        probs_again.astype(jnp.bfloat16),
        d_context,
        preferred_element_type=jnp.float32,
    )
    d_values = d_values.astype(jnp.bfloat16).reshape(count * LEN, D)
    d_scores = (
        probs_again * (d_probs - jnp.sum(probs_again * d_probs, axis=-1, keepdims=True))
    ).astype(jnp.bfloat16)
    d_queries = jnp.einsum(
        "bhqk,bkhd->bqhd", d_scores, key_rows, preferred_element_type=jnp.float32
    ) * HEAD_DIM ** (-0.5)
    d_queries = d_queries.astype(jnp.bfloat16).reshape(count * LEN, D)
    d_keys = jnp.einsum(
        "bhqk,bqhd->bkhd", d_scores, queries, preferred_element_type=jnp.float32
    ) * HEAD_DIM ** (-0.5)
    d_keys = d_keys.astype(jnp.bfloat16).reshape(count * LEN, D)
    d_query_mat = weight_grad(token_rows, d_queries)
    d_key_mat = weight_grad(token_rows, d_keys)
    d_value_mat = weight_grad(token_rows, d_values)
    d_query_bias = column_sum(d_queries)
    d_value_bias = column_sum(d_values)
    grad_rows = (
        d_resid_attn
        + project_back(d_queries, query_back)
        + project_back(d_keys, key_back)
        + project_back(d_values, value_back)
    )
    (
        grad_w_query,
        grad_w_key,
        grad_w_value,
        grad_w_output,
        grad_b_query,
        grad_b_value,
        grad_b_output,
        grad_gain_attn,
        grad_shift_attn,
    ) = (
        lax.psum_scatter(d_query_mat, "fsdp", scatter_dimension=0, tiled=True),
        lax.psum_scatter(d_key_mat, "fsdp", scatter_dimension=0, tiled=True),
        lax.psum_scatter(d_value_mat, "fsdp", scatter_dimension=0, tiled=True),
        lax.psum_scatter(d_output_mat, "fsdp", scatter_dimension=0, tiled=True),
        lax.psum_scatter(d_query_bias, "fsdp", scatter_dimension=0, tiled=True),
        lax.psum_scatter(d_value_bias, "fsdp", scatter_dimension=0, tiled=True),
        lax.psum_scatter(d_output_bias, "fsdp", scatter_dimension=0, tiled=True),
        lax.psum_scatter(d_attn_gain, "fsdp", scatter_dimension=0, tiled=True),
        lax.psum_scatter(d_attn_shift, "fsdp", scatter_dimension=0, tiled=True),
    )
    return (
        loss,
        block_out,
        grad_rows.reshape(count, LEN, D),
        grad_w_query,
        grad_w_key,
        grad_w_value,
        grad_w_output,
        grad_b_query,
        grad_b_value,
        grad_b_output,
        grad_gain_attn,
        grad_shift_attn,
        grad_w_inner,
        grad_b_inner,
        grad_w_outer,
        grad_b_outer,
        grad_gain_ffn,
        grad_shift_ffn,
    )


def solution(mesh):
    in_specs = (
        P("fsdp", None, None),
        P("fsdp"),
        P("fsdp"),
        P("fsdp", None, None),
        P("fsdp", None),
        P("fsdp", None),
        P("fsdp", None),
        P("fsdp", None),
        P("fsdp"),
        P("fsdp"),
        P("fsdp"),
        P("fsdp"),
        P("fsdp"),
        P("fsdp", None),
        P("fsdp"),
        P("fsdp", None),
        P("fsdp"),
        P("fsdp"),
        P("fsdp"),
    )
    out_specs = (
        P(),
        P("fsdp", None, None),
        P("fsdp", None, None),
        P("fsdp", None),
        P("fsdp", None),
        P("fsdp", None),
        P("fsdp", None),
        P("fsdp"),
        P("fsdp"),
        P("fsdp"),
        P("fsdp"),
        P("fsdp"),
        P("fsdp", None),
        P("fsdp"),
        P("fsdp", None),
        P("fsdp"),
        P("fsdp"),
        P("fsdp"),
    )
    return jax.shard_map(local, mesh=mesh, in_specs=in_specs, out_specs=out_specs, check_vma=False)
```

profile of v0, /device:TPU:0, one launch (start us, length us, event | category | flops | bytes accessed | tf_op | source)
XLA Modules:
  0.0 1316.2 jit_solution(8292508203558177508)
XLA Ops:
  19.5 42.6 %all-reduce.19 = (bf16[768]{0:T(1024)(128)(2,1)S(1)}, bf16[768]{0:T(1024)(128)(2,1)S(1)}, bf16[768]{0:T(1024)(128)(2,1)S(1)}, bf16[768]{0:T(1024)(128)(2,1)S(1)}...) all-reduce(bf16[768]{0:T(1024)(128)(2,1)S(1)} %dynamic-update-slice, ...), channel_id=1, replica_groups=mesh['fsdp'=32] {'fsdp'}, use_global_device_ids=true, to_apply=%add.1 | all-reduce | flops 9216 | bytes 36864
  62.2 5.6 all-gather.11.cloned.1.call-done
  67.8 3.1 convolution_convert_fusion.1
  70.9 3.9 reshape.305
  74.8 48.9 %all-gather.7.cloned.1.call-done = bf16[768,768]{1,0:T(8,128)(2,1)} async-done(((bf16[24,768]{1,0:T(8,128)(2,1)}), bf16[768,768]{1,0:T(8,128)(2,1)}) %all-gather.7.cloned.1.call-update) | async-done | bytes 1179664 | tf_op jit(solution)/shard_map/all_gather | solution.py:85
  123.7 2.7 add_convert_fusion.2
  126.4 3.9 reshape.307
  130.2 49.4 %all-gather.9.cloned.1.call-done = bf16[768,768]{1,0:T(8,128)(2,1)} async-done(((bf16[24,768]{1,0:T(8,128)(2,1)}), bf16[768,768]{1,0:T(8,128)(2,1)}) %all-gather.9.cloned.1.call-update) | async-done | bytes 1179664 | tf_op jit(solution)/shard_map/all_gather | solution.py:83
  179.6 2.7 add_convert_fusion.1
  182.3 3.9 reshape.308
  186.2 6.4 copy.101
  192.6 4.7 fusion.50
  197.3 1.9 fusion.6
  201.8 2.4 convert_bitcast_fusion.1
  204.3 2.4 copy.88
  206.7 3.2 reshape.269
  209.9 25.5 %all-gather.13.cloned.1.call-done = bf16[768,768]{1,0:T(8,128)(2,1)} async-done(((bf16[24,768]{1,0:T(8,128)(2,1)}), bf16[768,768]{1,0:T(8,128)(2,1)}) %all-gather.13.cloned.1.call-update) | async-done | bytes 1179664 | tf_op jit(solution)/shard_map/all_gather | solution.py:86
  235.4 3.8 fusion.51
  239.8 61.0 %all-gather.15.cloned.1.call-done = bf16[768,3072]{1,0:T(8,128)(2,1)} async-done(((bf16[24,3072]{1,0:T(8,128)(2,1)}), bf16[768,3072]{1,0:T(8,128)(2,1)}) %all-gather.15.cloned.1.call-update) | async-done | bytes 4718608 | tf_op jit(solution)/shard_map/all_gather | solution.py:125
  300.8 35.8 %multiply_convert_fusion = (bf16[1024,3072]{1,0:T(8,128)(2,1)}, f32[1024,3072]{1,0:T(8,128)}, f32[1024,3072]{1,0:T(8,128)}) fusion(f32[3072]{0:T(1024)S(1)} %convert_element_type.137, bf16[768,3072]{1,0:T(8,128)(2,1)} %all-gather.15.cloned.1.call-done, f32[1024,768]{1,0:T(8,128)S(1)} %get-tuple-element.132, f32[768]{0:T(1024)S(1)} %convert_element_type.135, ...), kind=kOutput, calls=%fused_computation.4 | convolution fusion | flops 5043388416 | bytes 39348224 | tf_op jit(solution)/shard_map/dot_general | solution.py:17
  336.6 29.4 %all-gather.17.cloned.1.call-done = bf16[3072,768]{1,0:T(8,128)(2,1)} async-done(((bf16[96,768]{1,0:T(8,128)(2,1)}), bf16[3072,768]{1,0:T(8,128)(2,1)}) %all-gather.17.cloned.1.call-update) | async-done | bytes 4718608 | tf_op jit(solution)/shard_map/all_gather | solution.py:127
  366.0 9.5 fusion.52
  376.0 2.8 fusion.44
  379.3 1.8 fusion.48
  381.4 44.2 %all_gather.71 = bf16[512,768]{1,0:T(8,128)(2,1)} all-gather(bf16[16,768]{1,0:T(8,128)(2,1)S(1)} %fusion.29), channel_id=1, replica_groups=mesh['fsdp'=32] {'fsdp'}, dimensions={0}, use_global_device_ids=true | all-gather | bytes 811008 | tf_op jit(solution)/shard_map/all_gather | solution.py:142
  425.6 2.8 reshape.271
  428.4 2.0 slice.38
  432.5 36.8 %psum.15 = f32[256]{0:T(256)S(1)} all-reduce(f32[256]{0:T(256)S(1)} %get-tuple-element.89), channel_id=1, replica_groups=mesh['fsdp'=32] {'fsdp'}, use_global_device_ids=true, to_apply=%region_13.14 | all-reduce | flops 256 | bytes 2048 | tf_op jit(solution)/shard_map/psum | solution.py:156
  471.8 4.1 copy_convert_fusion
  476.1 91.7 %reduce-scatter.14.cloned.1.call-done = f32[8,768]{1,0:T(8,128)} async-done(((f32[256,768]{1,0:T(8,128)}), f32[8,768]{1,0:T(8,128)}) %reduce-scatter.14.cloned.1.call-update) | async-done | bytes 24592 | tf_op jit(solution)/shard_map/reduce_scatter | solution.py:165
  570.3 3.7 copy.94
  575.0 1.8 fusion.46
  578.9 18.3 %convert_reduce_fusion = (f32[3072]{0:T(1024)S(1)}, bf16[1024,3072]{1,0:T(8,128)(2,1)}) fusion(f32[1024,3072]{1,0:T(8,128)} %get-tuple-element.126, bf16[1024,768]{1,0:T(8,128)(2,1)} %get-tuple-element.114, bf16[3072,768]{1,0:T(8,128)(2,1)} %all-gather.17.cloned.1.call-done, f32[1024,3072]{1,0:T(8,128)} %get-tuple-element.133, ...), kind=kOutput, calls=%fused_computation.2 | convolution fusion | flops 4885312512 | bytes 37773312 | tf_op jit(solution)/shard_map/dot_general | solution.py:21
  597.3 9.6 multiply_reduce_fusion.1
  611.0 2.8 fusion.56
  613.9 2.6 convolution_convert_fusion
  616.5 6.5 reshape.306
  623.0 10.5 multiply_reduce_fusion
  633.5 4.9 multiply_convert_fusion.3
  640.1 3.5 fusion.11
  643.6 4.2 copy.104
  647.8 3.2 reshape.278
  651.0 4.7 convolution_bitcast_fusion.1
  655.7 3.2 copy.116
  659.0 5.7 convert_reduce_fusion.2
  664.7 4.4 copy.100
  669.1 3.2 reshape.277
  672.3 3.3 convolution_bitcast_fusion.2
  675.6 2.0 copy.114
  677.6 7.7 convert_reduce_fusion.1
  685.3 4.2 copy.106
  689.5 3.2 reshape.279
  692.7 4.7 convolution_bitcast_fusion
  697.4 3.2 copy.118
  700.7 10.7 fusion.40
  712.8 10.4 fusion.57
  725.5 40.7 %all-reduce.18 = (f32[]{:T(128)}, f32[768]{0:T(1024)S(1)}, f32[768]{0:T(1024)S(1)}, f32[768]{0:T(1024)S(1)}, f32[768]{0:T(1024)S(1)}, /*index=5*/f32[768]{0:T(10...) all-reduce(f32[]{:T(128)S(6)} %sub.93, ...), channel_id=1, replica_groups=mesh['fsdp'=32] {'fsdp'}, use_global_device_ids=true, to_apply=%region_11.12 | all-reduce | flops 9217 | bytes 73736 | tf_op jit(solution)/shard_map/psum | solution.py:156
  772.8 3.4 fusion.55
  778.9 3.6 add_add_fusion.2
  782.5 34.2 %reduce-scatter.24.cloned.1.call-done = f32[24,768]{1,0:T(8,128)} async-done(((f32[768,768]{1,0:T(8,128)}), f32[24,768]{1,0:T(8,128)}) %reduce-scatter.24.cloned.1.call-update) | async-done | bytes 73744
  816.7 103.8 %reduce-scatter.22.cloned.1.call-done = f32[24,768]{1,0:T(8,128)} async-done(((f32[768,768]{1,0:T(8,128)}), f32[24,768]{1,0:T(8,128)}) %reduce-scatter.22.cloned.1.call-update) | async-done | bytes 73744
  920.6 104.8 %reduce-scatter.26.cloned.1.call-done = f32[24,768]{1,0:T(8,128)} async-done(((f32[768,768]{1,0:T(8,128)}), f32[24,768]{1,0:T(8,128)}) %reduce-scatter.26.cloned.1.call-update) | async-done | bytes 73744
  1025.3 140.8 %reduce-scatter.18.cloned.1.call-done = f32[24,3072]{1,0:T(8,128)} async-done(((f32[768,3072]{1,0:T(8,128)}), f32[24,3072]{1,0:T(8,128)}) %reduce-scatter.18.cloned.1.call-update) | async-done | bytes 294928 | tf_op jit(solution)/shard_map/reduce_scatter | solution.py:188
  1166.2 142.1 %reduce-scatter.20.cloned.1.call-done = f32[96,768]{1,0:T(8,128)} async-done(((f32[3072,768]{1,0:T(8,128)}), f32[96,768]{1,0:T(8,128)}) %reduce-scatter.20.cloned.1.call-update) | async-done | bytes 294928 | tf_op jit(solution)/shard_map/reduce_scatter | solution.py:190
  (170 shorter events, 43.0 us)
Async XLA Ops:
  7.2 60.6 %all-gather.11.cloned.1.call-start = ((), (), s32[]{:S(2)}) async-start(), calls=%async_computation.9 | async-start | bytes 1216512 | tf_op jit(solution)/shard_map/all_gather | solution.py:84
  7.9 115.8 %all-gather.7.cloned.1.call-start = ((), (), s32[]{:S(2)}) async-start(), calls=%async_computation.7 | async-start | bytes 1216512 | tf_op jit(solution)/shard_map/all_gather | solution.py:85
  8.7 171.0 %all-gather.9.cloned.1.call-start = ((), (), s32[]{:S(2)}) async-start(), calls=%async_computation.8 | async-start | bytes 1216512 | tf_op jit(solution)/shard_map/all_gather | solution.py:83
  9.4 226.0 %all-gather.13.cloned.1.call-start = ((), (), s32[]{:S(2)}) async-start(), calls=%async_computation.10 | async-start | bytes 1216512 | tf_op jit(solution)/shard_map/all_gather | solution.py:86
  10.0 290.8 %all-gather.15.cloned.1.call-start = ((), (), s32[]{:S(2)}) async-start(), calls=%async_computation.11 | async-start | bytes 4866048 | tf_op jit(solution)/shard_map/all_gather | solution.py:125
  10.6 355.4 %all-gather.17.cloned.1.call-start = ((), (), s32[]{:S(2)}) async-start(), calls=%async_computation.12 | async-start | bytes 4866048 | tf_op jit(solution)/shard_map/all_gather | solution.py:127
  11.1 556.6 %reduce-scatter.14.cloned.1.call-start = ((), (), s32[]{:S(2)}) async-start(), calls=%async_computation.13 | async-start | bytes 811008 | tf_op jit(solution)/shard_map/reduce_scatter | solution.py:165
  70.9 52.8 %copy-start.28 = (bf16[16,64,768]{2,1,0:T(8,128)(2,1)S(1)}, bf16[16,64,768]{2,1,0:T(8,128)(2,1)}, u32[]{:S(2)}) copy-start(bf16[16,64,768]{2,1,0:T(8,128)(2,1)} %param.21) | copy-start | bytes 4718596
  192.6 4.7 copy-start.5
  197.3 3.2 copy-start
  197.3 3.2 copy-start.18
  197.3 4.5 copy-start.9
  201.8 2.4 copy-start.23
  239.2 97.3 %copy-start.1 = (f32[1024,768]{1,0:T(8,128)}, f32[1024,768]{1,0:T(8,128)S(1)}, u32[]{:S(2)}) copy-start(f32[1024,768]{1,0:T(8,128)S(1)} %get-tuple-element.132) | copy-start | bytes 9437188
  239.8 96.8 %copy-start.25 = (f32[1024]{0:T(1024)}, f32[1024]{0:T(1024)S(1)}, u32[]{:S(2)}) copy-start(f32[1024]{0:T(1024)S(1)} %multiply_reduce_fusion.5) | copy-start | bytes 12292
  378.8 52.6 %copy-start.27 = (s32[8]{0:T(128)S(1)}, s32[8]{0:T(128)}, u32[]{:S(2)}) copy-start(s32[8]{0:T(128)} %param.23) | copy-start | bytes 100
  430.5 0.9 copy-start.21
  471.8 310.7 %reduce-scatter.16.cloned.1.call-start = ((), (), s32[]{:S(2)}) async-start(), calls=%async_computation.14 | async-start | bytes 2433024 | tf_op jit(solution)/shard_map/reduce_scatter | solution.py:256
  471.8 4.1 copy-start.22
  576.8 2.1 copy-start.10
  578.9 18.3 %copy-start.2 = (f32[1024,768]{1,0:T(8,128)S(1)}, f32[1024,768]{1,0:T(8,128)}, u32[]{:S(2)}) copy-start(f32[1024,768]{1,0:T(8,128)} %copy-done.1) | copy-start | bytes 9437188
  578.9 18.3 %copy-start.11 = (f32[1024,768]{1,0:T(8,128)S(1)}, f32[1024,768]{1,0:T(8,128)}, u32[]{:S(2)}) copy-start(f32[1024,768]{1,0:T(8,128)} %copy-done.10) | copy-start | bytes 9437188
  597.2 9.6 copy-start.26
  608.4 1.6 copy-start.7
  608.4 2.5 copy-start.15
  611.0 2.9 copy-start.19
  611.0 2.9 copy-start.24
  611.0 2.9 copy-start.30
  613.8 202.9 %reduce-scatter.24.cloned.1.call-start = ((), (), s32[]{:S(2)}) async-start(), calls=%async_computation.18 | async-start | bytes 2433024
  616.5 17.0 %slice-start = ((s8[6291456]{0:T(1024)(128)(4,1)}), s8[2097152]{0:T(1024)(128)(4,1)S(1)}, s32[]{:S(2)}) async-start(s8[6291456]{0:T(1024)(128)(4,1)} %bitcast.113), calls=%async_computation.20 | async-start | bytes 4194304
  623.0 10.6 slice-start.1
  633.5 6.6 copy-start.6
  638.4 1.7 copy-start.12
  655.7 3.3 copy-start.13
  658.9 261.6 %reduce-scatter.22.cloned.1.call-start = ((), (), s32[]{:S(2)}) async-start(), calls=%async_computation.17 | async-start | bytes 2433024
  677.6 347.8 %reduce-scatter.26.cloned.1.call-start = ((), (), s32[]{:S(2)}) async-start(), calls=%async_computation.19 | async-start | bytes 2433024
  697.4 3.3 copy-start.3
  700.6 465.5 %reduce-scatter.18.cloned.1.call-start = ((), (), s32[]{:S(2)}) async-start(), calls=%async_computation.15 | async-start | bytes 9732096 | tf_op jit(solution)/shard_map/reduce_scatter | solution.py:188
  711.4 1.4 copy-start.17
  711.4 596.9 %reduce-scatter.20.cloned.1.call-start = ((), (), s32[]{:S(2)}) async-start(), calls=%async_computation.16 | async-start | bytes 9732096 | tf_op jit(solution)/shard_map/reduce_scatter | solution.py:190
  723.1 1.9 copy-start.4
  772.8 3.4 copy-start.16
  772.8 3.4 copy-start.29
  776.1 1.9 copy-start.8
  776.1 2.4 copy-start.14
  776.2 2.8 copy-start.20
Sparse Core Ops, SparseCore 0:
  10.9 56.8 all-gather.10
  70.7 53.0 all-gather.6
  126.6 52.9 all-gather.8
  182.4 52.9 all-gather.12
  238.1 62.5 all-gather.14
  303.5 62.4 all-gather.16
  471.9 95.8 reduce-scatter.13
  613.9 98.0 reduce-scatter.15
  718.7 97.9 reduce-scatter.23
  822.4 98.0 reduce-scatter.21
  927.3 98.0 reduce-scatter.25
  1031.7 134.4 reduce-scatter.17
  1173.6 134.5 reduce-scatter.19
where the time goes:
time: 1330 us; the launch traced here: 1320 us
  waiting for transfers between devices  841 us (63%)
  matrix products  169 us (13%)
  blocking collectives  164 us (12%)
  local copies, waits for them, and re-layouts  95.5 us (7%)
  other arithmetic  26.6 us (2%)
  between operations  18.8 us (1%)
    unnamed x16, waiting for transfers between devices  247 us
    reduce_scatter x1, waiting for transfers between devices, local(): lax.psum_scatter(d_outer_mat, 'fsdp', scatter_dimension=0, tiled=True)  142 us
    reduce_scatter x1, waiting for transfers between devices, local(): lax.psum_scatter(d_inner_mat, 'fsdp', scatter_dimension=0, tiled=True)  141 us
    reduce_scatter x1, waiting for transfers between devices, local(): lax.psum_scatter(target_part, 'fsdp', scatter_dimension=0, tiled=True)  91.7 us
    psum x2, blocking collectives, local(): col_total, loss_total = lax.psum((col_part, local_loss), 'fsdp')  77.6 us
    all_gather x1, waiting for transfers between devices, local(): lax.all_gather(w_inner, 'fsdp', axis=0, tiled=True)  61 us
    dot_general x7, matrix products, project(): return jnp.dot(rows, weight, preferred_element_type=jnp.float32)  57.8 us
    all_gather x1, waiting for transfers between devices, local(): lax.all_gather(w_query, 'fsdp', axis=0, tiled=True)  49.4 us
  transfers between devices with their start and end apart: 13, of which 12 were waited for; matrix products, arithmetic and copies ran while one was open for 16% of the time, Pallas kernels for 0%

commit v1 on v0

--- a/solution.py
+++ b/solution.py
@@ -11,6 +11,25 @@
 pool_eps = 1e-06
 sim_scale = 50.0
 sim_margin = 0.3
+
+
+def advance_the_units(base_x, dim_i):
+    f_now = list(base_x.shape[1:])
+    f_now[dim_i] *= base_x.shape[0]
+    value_now = jnp.moveaxis(base_x, 0, dim_i).reshape(f_now)
+    return value_now
+
+
+def loads_store(x_in, across):
+    n_all = lax.axis_size(across)
+    passed = x_in[None]
+    for idx in range(n_all.bit_length() - 1):
+        r_now = 1 << idx
+        m_next = lax.ppermute(passed, axis_name=across, perm=[(t, t ^ r_now) for t in range(n_all)])
+        out_arr = jnp.stack([passed, m_next])
+        x_next = lax.axis_index(across) >> idx & 1
+        passed = jnp.where(x_next == 0, out_arr, out_arr[::-1]).reshape(-1, *x_in.shape)
+    return passed
 
 
 def project(rows, weight):
@@ -139,7 +158,7 @@
     cls_rows = block_rows.reshape(count, LEN, D)[:, 0, :]
     unit, pool_back = jax.vjp(normalize, cls_rows)
     unit_low = unit.astype(jnp.bfloat16)
-    every_unit = lax.all_gather(unit_low, "fsdp", axis=0, tiled=True)
+    every_unit = advance_the_units(loads_store(unit_low, "fsdp"), 0)
     every_pair = every_unit.reshape(every_unit.shape[0] // 2, 2, D)
     all_targets = every_pair[:, 1, :]
     own_pair = unit_low.reshape(half, 2, D)

time: 1330 us -> 1320 us (level)
  blocking collectives: 164 us -> 121 us
  waiting for transfers between devices: 841 us -> 868 us
    all_gather x1 -> x0, blocking collectives: 44.2 us -> none  [local(): every_unit = lax.all_gather(unit_low, 'fsdp', axis=0, tiled=True)]
    ppermute x0 -> x5, waiting for transfers between devices: none -> 25.8 us  [loads_store(): lax.ppermute(passed, axis_name=across, perm=[(t, t ^ r_now) for t in rang...]
  transfers between devices with their start and end apart: 13 -> 18, of which waited for: 12 -> 17; matrix products, arithmetic and copies ran while one was open for 16% -> 16% of each run, Pallas kernels for 0% -> 0%
where the time goes in v1:
time: 1320 us; the launch traced here: 1310 us
  waiting for transfers between devices  868 us (66%)
  matrix products  169 us (13%)
  blocking collectives  121 us (9%)
  local copies, waits for them, and re-layouts  95.6 us (7%)
  other arithmetic  30.9 us (2%)
  between operations  18.9 us (1%)
    unnamed x16, waiting for transfers between devices  246 us
    reduce_scatter x1, waiting for transfers between devices, local(): lax.psum_scatter(d_outer_mat, 'fsdp', scatter_dimension=0, tiled=True)  142 us
    reduce_scatter x1, waiting for transfers between devices, local(): lax.psum_scatter(d_inner_mat, 'fsdp', scatter_dimension=0, tiled=True)  141 us
    reduce_scatter x1, waiting for transfers between devices, local(): lax.psum_scatter(target_part, 'fsdp', scatter_dimension=0, tiled=True)  92.7 us
    psum x2, blocking collectives, local(): col_total, loss_total = lax.psum((col_part, local_loss), 'fsdp')  78.2 us
    all_gather x1, waiting for transfers between devices, local(): lax.all_gather(w_inner, 'fsdp', axis=0, tiled=True)  61 us
    dot_general x7, matrix products, project(): return jnp.dot(rows, weight, preferred_element_type=jnp.float32)  57.7 us
    all_gather x1, waiting for transfers between devices, local(): lax.all_gather(w_query, 'fsdp', axis=0, tiled=True)  49.4 us
  transfers between devices with their start and end apart: 18, of which 17 were waited for; matrix products, arithmetic and copies ran while one was open for 16% of the time, Pallas kernels for 0%

profile of v1, /device:TPU:0, one launch (start us, length us, event | category | flops | bytes accessed | tf_op | source)
XLA Modules:
  0.0 1311.0 jit_solution(8403193185703098504)
XLA Ops:
  19.5 42.6 %all-reduce.19 = (bf16[768]{0:T(1024)(128)(2,1)S(1)}, bf16[768]{0:T(1024)(128)(2,1)S(1)}, bf16[768]{0:T(1024)(128)(2,1)S(1)}, bf16[768]{0:T(1024)(128)(2,1)S(1)}...) all-reduce(bf16[768]{0:T(1024)(128)(2,1)S(1)} %dynamic-update-slice, ...), channel_id=1, replica_groups=mesh['fsdp'=32] {'fsdp'}, use_global_device_ids=true, to_apply=%add.1 | all-reduce | flops 9216 | bytes 36864
  62.1 5.6 all-gather.11.cloned.1.call-done
  67.8 3.1 convolution_convert_fusion.1
  70.9 3.9 reshape.381
  74.8 48.9 %all-gather.7.cloned.1.call-done = bf16[768,768]{1,0:T(8,128)(2,1)} async-done(((bf16[24,768]{1,0:T(8,128)(2,1)}), bf16[768,768]{1,0:T(8,128)(2,1)}) %all-gather.7.cloned.1.call-update) | async-done | bytes 1179664 | tf_op jit(solution)/shard_map/all_gather | solution.py:104
  123.7 2.7 add_convert_fusion.2
  126.4 3.9 reshape.383
  130.2 49.4 %all-gather.9.cloned.1.call-done = bf16[768,768]{1,0:T(8,128)(2,1)} async-done(((bf16[24,768]{1,0:T(8,128)(2,1)}), bf16[768,768]{1,0:T(8,128)(2,1)}) %all-gather.9.cloned.1.call-update) | async-done | bytes 1179664 | tf_op jit(solution)/shard_map/all_gather | solution.py:102
  179.6 2.7 add_convert_fusion.1
  182.3 3.9 reshape.384
  186.2 6.4 copy.127
  192.6 4.7 fusion.57
  201.8 2.4 convert_bitcast_fusion.1
  204.3 2.4 copy.115
  206.7 3.2 reshape.342
  209.9 25.5 %all-gather.13.cloned.1.call-done = bf16[768,768]{1,0:T(8,128)(2,1)} async-done(((bf16[24,768]{1,0:T(8,128)(2,1)}), bf16[768,768]{1,0:T(8,128)(2,1)}) %all-gather.13.cloned.1.call-update) | async-done | bytes 1179664 | tf_op jit(solution)/shard_map/all_gather | solution.py:105
  235.4 3.8 fusion.58
  239.8 61.0 %all-gather.15.cloned.1.call-done = bf16[768,3072]{1,0:T(8,128)(2,1)} async-done(((bf16[24,3072]{1,0:T(8,128)(2,1)}), bf16[768,3072]{1,0:T(8,128)(2,1)}) %all-gather.15.cloned.1.call-update) | async-done | bytes 4718608 | tf_op jit(solution)/shard_map/all_gather | solution.py:144
  300.8 35.8 %multiply_convert_fusion = (bf16[1024,3072]{1,0:T(8,128)(2,1)}, f32[1024,3072]{1,0:T(8,128)}, f32[1024,3072]{1,0:T(8,128)}) fusion(f32[3072]{0:T(1024)S(1)} %convert_element_type.153, bf16[768,3072]{1,0:T(8,128)(2,1)} %all-gather.15.cloned.1.call-done, f32[1024,768]{1,0:T(8,128)S(1)} %get-tuple-element.152, f32[768]{0:T(1024)S(1)} %convert_element_type.151, ...), kind=kOutput, calls=%fused_computation.4 | convolution fusion | flops 5043388416 | bytes 39348224 | tf_op jit(solution)/shard_map/dot_general | solution.py:36
  336.5 29.4 %all-gather.17.cloned.1.call-done = bf16[3072,768]{1,0:T(8,128)(2,1)} async-done(((bf16[96,768]{1,0:T(8,128)(2,1)}), bf16[3072,768]{1,0:T(8,128)(2,1)}) %all-gather.17.cloned.1.call-update) | async-done | bytes 4718608 | tf_op jit(solution)/shard_map/all_gather | solution.py:146
  366.0 9.5 fusion.59
  375.9 2.8 fusion.51
  383.9 2.7 collective-permute-done.1
  388.2 3.1 collective-permute-done.2
  393.4 3.9 collective-permute-done.3
  399.0 2.1 collective-permute-start.4
  401.4 15.3 %collective-permute-done.4 = bf16[16,16,768]{2,1,0:T(8,128)(2,1)} collective-permute-done((bf16[16,16,768]{2,1,0:T(8,128)(2,1)}, bf16[16,16,768]{2,1,0:T(8,128)(2,1)}, u32[]{:S(2)}, u32[]{:S(2)}) %collective-permute-start.4) | collective-permute-done | bytes 393248 | tf_op jit(solution)/shard_map/ppermute | solution.py:28
  418.9 2.8 reshape_reshape_reshape.3
  421.8 2.0 slice.38
  425.8 37.3 %psum.15 = f32[256]{0:T(256)S(1)} all-reduce(f32[256]{0:T(256)S(1)} %get-tuple-element.107), channel_id=1, replica_groups=mesh['fsdp'=32] {'fsdp'}, use_global_device_ids=true, to_apply=%region_13.14 | all-reduce | flops 256 | bytes 2048 | tf_op jit(solution)/shard_map/psum | solution.py:175
  465.6 4.1 copy_convert_fusion
  469.9 92.7 %reduce-scatter.14.cloned.1.call-done = f32[8,768]{1,0:T(8,128)} async-done(((f32[256,768]{1,0:T(8,128)}), f32[8,768]{1,0:T(8,128)}) %reduce-scatter.14.cloned.1.call-update) | async-done | bytes 24592 | tf_op jit(solution)/shard_map/reduce_scatter | solution.py:184
  565.0 3.7 copy.120
  573.7 18.3 %convert_reduce_fusion = (f32[3072]{0:T(1024)S(1)}, bf16[1024,3072]{1,0:T(8,128)(2,1)}) fusion(f32[1024,3072]{1,0:T(8,128)} %get-tuple-element.144, bf16[1024,768]{1,0:T(8,128)(2,1)} %get-tuple-element.132, bf16[3072,768]{1,0:T(8,128)(2,1)} %all-gather.17.cloned.1.call-done, f32[1024,3072]{1,0:T(8,128)} %get-tuple-element.153, ...), kind=kOutput, calls=%fused_computation.2 | convolution fusion | flops 4885312512 | bytes 37773312 | tf_op jit(solution)/shard_map/dot_general | solution.py:40
  592.0 9.6 multiply_reduce_fusion.1
  605.7 2.8 fusion.63
  608.7 2.6 convolution_convert_fusion
  611.2 6.5 reshape.382
  617.7 10.5 multiply_reduce_fusion
  628.3 4.9 multiply_convert_fusion.3
  634.8 3.5 fusion.11
  638.3 4.2 copy.130
  642.6 3.2 reshape.354
  645.8 4.7 convolution_bitcast_fusion.1
  650.5 3.2 copy.142
  653.7 5.7 convert_reduce_fusion.2
  659.4 4.4 copy.126
  663.8 3.2 reshape.353
  667.0 3.3 convolution_bitcast_fusion.2
  672.4 7.7 convert_reduce_fusion.1
  680.0 4.2 copy.132
  684.3 3.2 reshape.355
  687.4 4.7 convolution_bitcast_fusion
  692.1 3.2 copy.144
  695.4 10.6 fusion.47
  707.5 10.4 fusion.64
  720.2 40.9 %all-reduce.18 = (f32[]{:T(128)}, f32[768]{0:T(1024)S(1)}, f32[768]{0:T(1024)S(1)}, f32[768]{0:T(1024)S(1)}, f32[768]{0:T(1024)S(1)}, /*index=5*/f32[768]{0:T(10...) all-reduce(f32[]{:T(128)S(6)} %sub.93, ...), channel_id=1, replica_groups=mesh['fsdp'=32] {'fsdp'}, use_global_device_ids=true, to_apply=%region_11.12 | all-reduce | flops 9217 | bytes 73736 | tf_op jit(solution)/shard_map/psum | solution.py:175
  767.7 3.3 fusion.62
  773.8 3.6 add_add_fusion.2
  777.4 34.2 %reduce-scatter.24.cloned.1.call-done = f32[24,768]{1,0:T(8,128)} async-done(((f32[768,768]{1,0:T(8,128)}), f32[24,768]{1,0:T(8,128)}) %reduce-scatter.24.cloned.1.call-update) | async-done | bytes 73744
  811.6 103.7 %reduce-scatter.22.cloned.1.call-done = f32[24,768]{1,0:T(8,128)} async-done(((f32[768,768]{1,0:T(8,128)}), f32[24,768]{1,0:T(8,128)}) %reduce-scatter.22.cloned.1.call-update) | async-done | bytes 73744
  915.3 104.8 %reduce-scatter.26.cloned.1.call-done = f32[24,768]{1,0:T(8,128)} async-done(((f32[768,768]{1,0:T(8,128)}), f32[24,768]{1,0:T(8,128)}) %reduce-scatter.26.cloned.1.call-update) | async-done | bytes 73744
  1020.1 140.9 %reduce-scatter.18.cloned.1.call-done = f32[24,3072]{1,0:T(8,128)} async-done(((f32[768,3072]{1,0:T(8,128)}), f32[24,3072]{1,0:T(8,128)}) %reduce-scatter.18.cloned.1.call-update) | async-done | bytes 294928 | tf_op jit(solution)/shard_map/reduce_scatter | solution.py:207
  1161.0 142.1 %reduce-scatter.20.cloned.1.call-done = f32[96,768]{1,0:T(8,128)} async-done(((f32[3072,768]{1,0:T(8,128)}), f32[96,768]{1,0:T(8,128)}) %reduce-scatter.20.cloned.1.call-update) | async-done | bytes 294928 | tf_op jit(solution)/shard_map/reduce_scatter | solution.py:209
  (190 shorter events, 60.9 us)
Async XLA Ops:
  7.2 60.6 %all-gather.11.cloned.1.call-start = ((), (), s32[]{:S(2)}) async-start(), calls=%async_computation.9 | async-start | bytes 1216512 | tf_op jit(solution)/shard_map/all_gather | solution.py:103
  7.9 115.8 %all-gather.7.cloned.1.call-start = ((), (), s32[]{:S(2)}) async-start(), calls=%async_computation.7 | async-start | bytes 1216512 | tf_op jit(solution)/shard_map/all_gather | solution.py:104
  8.7 171.0 %all-gather.9.cloned.1.call-start = ((), (), s32[]{:S(2)}) async-start(), calls=%async_computation.8 | async-start | bytes 1216512 | tf_op jit(solution)/shard_map/all_gather | solution.py:102
  9.4 226.0 %all-gather.13.cloned.1.call-start = ((), (), s32[]{:S(2)}) async-start(), calls=%async_computation.10 | async-start | bytes 1216512 | tf_op jit(solution)/shard_map/all_gather | solution.py:105
  10.0 290.8 %all-gather.15.cloned.1.call-start = ((), (), s32[]{:S(2)}) async-start(), calls=%async_computation.11 | async-start | bytes 4866048 | tf_op jit(solution)/shard_map/all_gather | solution.py:144
  10.6 355.4 %all-gather.17.cloned.1.call-start = ((), (), s32[]{:S(2)}) async-start(), calls=%async_computation.12 | async-start | bytes 4866048 | tf_op jit(solution)/shard_map/all_gather | solution.py:146
  11.1 551.4 %reduce-scatter.14.cloned.1.call-start = ((), (), s32[]{:S(2)}) async-start(), calls=%async_computation.13 | async-start | bytes 811008 | tf_op jit(solution)/shard_map/reduce_scatter | solution.py:184
  70.9 52.8 %copy-start.28 = (bf16[16,64,768]{2,1,0:T(8,128)(2,1)S(1)}, bf16[16,64,768]{2,1,0:T(8,128)(2,1)}, u32[]{:S(2)}) copy-start(bf16[16,64,768]{2,1,0:T(8,128)(2,1)} %param.21) | copy-start | bytes 4718596
  192.6 4.7 copy-start.5
  197.3 3.2 copy-start
  197.3 3.2 copy-start.18
  197.3 4.5 copy-start.9
  201.8 2.4 copy-start.23
  239.2 97.3 %copy-start.1 = (f32[1024,768]{1,0:T(8,128)}, f32[1024,768]{1,0:T(8,128)S(1)}, u32[]{:S(2)}) copy-start(f32[1024,768]{1,0:T(8,128)S(1)} %get-tuple-element.152) | copy-start | bytes 9437188
  239.8 96.8 %copy-start.25 = (f32[1024]{0:T(1024)}, f32[1024]{0:T(1024)S(1)}, u32[]{:S(2)}) copy-start(f32[1024]{0:T(1024)S(1)} %multiply_reduce_fusion.5) | copy-start | bytes 12292
  381.2 1.2 collective-permute-start
  382.5 4.2 collective-permute-start.1
  386.6 4.7 collective-permute-start.2
  391.4 5.8 collective-permute-start.3
  399.0 17.6 %collective-permute-start.4 = (bf16[16,16,768]{2,1,0:T(8,128)(2,1)}, bf16[16,16,768]{2,1,0:T(8,128)(2,1)}, u32[]{:S(2)}, u32[]{:S(2)}) collective-permute-start(bf16[16,16,768]{2,1,0:T(8,128)(2,1)} %bitcast.17), channel_id=1, source_target_pairs={{0,16},{1,17},{2,18},{3,19},{4,20},{5,21},{6,22},{7,23},{8,24},{9,... | collective-permute-start | bytes 1179656 | tf_op jit(solution)/shard_map/ppermute | solution.py:28
  416.7 8.0 copy-start.27
  423.8 0.9 copy-start.21
  465.5 311.9 %reduce-scatter.16.cloned.1.call-start = ((), (), s32[]{:S(2)}) async-start(), calls=%async_computation.14 | async-start | bytes 2433024 | tf_op jit(solution)/shard_map/reduce_scatter | solution.py:275
  465.6 4.1 copy-start.22
  571.5 2.1 copy-start.10
  573.7 18.3 %copy-start.2 = (f32[1024,768]{1,0:T(8,128)S(1)}, f32[1024,768]{1,0:T(8,128)}, u32[]{:S(2)}) copy-start(f32[1024,768]{1,0:T(8,128)} %copy-done.1) | copy-start | bytes 9437188
  573.7 18.3 %copy-start.11 = (f32[1024,768]{1,0:T(8,128)S(1)}, f32[1024,768]{1,0:T(8,128)}, u32[]{:S(2)}) copy-start(f32[1024,768]{1,0:T(8,128)} %copy-done.10) | copy-start | bytes 9437188
  592.0 9.6 copy-start.26
  603.2 1.6 copy-start.7
  603.2 2.5 copy-start.15
  605.7 2.9 copy-start.19
  605.7 2.9 copy-start.24
  605.7 2.9 copy-start.30
  608.5 203.0 %reduce-scatter.24.cloned.1.call-start = ((), (), s32[]{:S(2)}) async-start(), calls=%async_computation.18 | async-start | bytes 2433024
  611.2 17.0 %slice-start = ((s8[6291456]{0:T(1024)(128)(4,1)}), s8[2097152]{0:T(1024)(128)(4,1)S(1)}, s32[]{:S(2)}) async-start(s8[6291456]{0:T(1024)(128)(4,1)} %bitcast.136), calls=%async_computation.20 | async-start | bytes 4194304
  617.7 10.6 slice-start.1
  628.3 6.6 copy-start.6
  633.1 1.7 copy-start.12
  650.5 3.3 copy-start.13
  653.7 261.6 %reduce-scatter.22.cloned.1.call-start = ((), (), s32[]{:S(2)}) async-start(), calls=%async_computation.17 | async-start | bytes 2433024
  672.3 347.8 %reduce-scatter.26.cloned.1.call-start = ((), (), s32[]{:S(2)}) async-start(), calls=%async_computation.19 | async-start | bytes 2433024
  692.1 3.3 copy-start.3
  695.4 465.6 %reduce-scatter.18.cloned.1.call-start = ((), (), s32[]{:S(2)}) async-start(), calls=%async_computation.15 | async-start | bytes 9732096 | tf_op jit(solution)/shard_map/reduce_scatter | solution.py:207
  706.1 1.4 copy-start.17
  706.1 597.0 %reduce-scatter.20.cloned.1.call-start = ((), (), s32[]{:S(2)}) async-start(), calls=%async_computation.16 | async-start | bytes 9732096 | tf_op jit(solution)/shard_map/reduce_scatter | solution.py:209
  717.9 1.9 copy-start.4
  767.7 3.4 copy-start.16
  767.7 3.4 copy-start.29
  771.0 2.0 copy-start.8
  771.1 2.4 copy-start.14
  771.1 2.8 copy-start.20
Sparse Core Ops, SparseCore 0:
  10.9 56.8 all-gather.10
  70.7 53.0 all-gather.6
  126.6 52.9 all-gather.8
  182.4 52.9 all-gather.12
  238.1 62.5 all-gather.14
  303.5 62.4 all-gather.16
  465.6 96.8 reduce-scatter.13
  608.7 98.0 reduce-scatter.15
  713.5 98.0 reduce-scatter.23
  817.3 97.9 reduce-scatter.21
  922.0 98.0 reduce-scatter.25
  1026.4 134.5 reduce-scatter.17
  1168.5 134.5 reduce-scatter.19
